TPU v7x, 32 devices: a whole 2x2x4 slice. The times are simulated.
32 devices in a mesh: grp: 4 (over y, x), word: 8 (over z, core).
Axes of the slice: x: 2, y: 2, z: 4, core: 2. Of those that a mesh axis runs over, the one named last changes fastest.
Arguments:
- descriptors: bfloat16 [262144, 128], P(('grp', 'word'))
- word_ids: int32 [262144], P(('grp', 'word')), may hold values from 0 to 1023, as said below
Outputs:
- centroids: bfloat16 [1024, 128], P('word')
- nearest: float32 [262144], P(('grp', 'word'))
Inputs may be any that keep to these rules, and one draw needn't show every extreme that they name: `word_ids`: the word ids of one device's descriptors lie in a window of 64 consecutive ids, counted modulo 1024; every word id from 0 to 1023 occurs at least once.
All inputs are finite; a program needn't handle non-finite values.
Results may differ from a plain program's by a relative error of at most 0.0015.
Values may be sent and summed in bfloat16 or wider, within the bound.
No kernel may reach another device: no remote copies, remote signals or barrier semaphores. Data moves between devices by JAX's collectives and lax.ppermute only.
A program may use at most 64 MiB of HBM per device.

v0:
```python
import jax
import jax.numpy as jnp
from jax import lax
from jax.sharding import PartitionSpec as P

K = 1024


def local_sums(descriptors, word_ids):
    rows = descriptors.shape[0]
    depth = descriptors.shape[1]
    words = K
    block = min(1024, rows)
    xs = descriptors.reshape(rows // block, block, depth)
    idx = word_ids.reshape(rows // block, block)
    table = lax.broadcasted_iota(jnp.int32, (1, words), 1)

    def step(carry, item):
        total, count = carry
        xb, ib = item
        onehot = (ib[:, None] == table).astype(jnp.bfloat16)
        total = total + jnp.einsum("nk,nd->kd", onehot, xb, preferred_element_type=jnp.float32)
        count = count + jnp.sum(onehot.astype(jnp.float32), axis=0)
        return ((total, count), None)

    init = (jnp.zeros((words, depth), jnp.float32), jnp.zeros((words,), jnp.float32))
    (total, count), unused = lax.scan(step, init, (xs, idx))
    return (total, count)


def on_device(descriptors, word_ids):
    total, count = local_sums(descriptors, word_ids)
    xf = descriptors.astype(jnp.float32)
    xnorm = jnp.sum(xf * xf, axis=1)
    depth = descriptors.shape[1]
    start_min = jnp.full(xnorm.shape, jnp.inf, jnp.float32)
    total, count = lax.psum((total, count), ("grp", "word"))
    whole = (total / count[:, None]).astype(jnp.bfloat16)
    pf = whole.astype(jnp.float32)
    cnorm = jnp.sum(pf * pf, axis=1)
    dots = jnp.dot(descriptors, whole.T, preferred_element_type=jnp.float32)
    dist = (xnorm[:, None] - 2.0 * dots + cnorm[None, :]) / depth
    nearest = jnp.minimum(start_min, jnp.min(dist, axis=1))
    owned_rows = whole.shape[0] // lax.axis_size("word")
    begin = lax.axis_index("word") * owned_rows
    cent = lax.dynamic_slice_in_dim(whole, begin, owned_rows, 0)
    return (cent, nearest)


def solution(mesh):
    return jax.shard_map(
        on_device,
        mesh=mesh,
        in_specs=(P(("grp", "word"), None), P(("grp", "word"))),
        out_specs=(P("word", None), P(("grp", "word"))),
        check_vma=False,
    )
```

profile of v0, /device:TPU:0, one launch (start us, length us, event | category | flops | bytes accessed | tf_op | source)
XLA Modules:
  0.0 181.5 jit_solution(9641654276949608156)
XLA Ops:
  7.2 0.0 all-reduce.2.cloned.1.call-start
  7.2 0.8 reshape.15
  8.0 24.5 %while.13 = (s32[]{:T(128)}, f32[1024,128]{1,0:T(8,128)S(1)}, f32[1024]{0:T(1024)S(1)}, s32[8,1024]{1,0:T(8,128)S(1)}, bf16[8,1024,128]{2,1,0:T(8,128)(2,1)}, /*index=5*/s32[]{:T(128)}, s32[]{:T(128)}) while((s32[]{:T(128)}, f32[1024,128]{1,0:T(8,128)S(1)}, f32[1024]{0:T(1024)S(1)}, s32[8,1024]{1,0:T(8,128)S(1)}, ...), condition=%wide.region_2.3_spmd.clone, body=%wide.region_0.2_spmd.clone.sunk | while | flops 273941504 | bytes 1343592 | solution.py:27
  8.0 2.5 %fusion.14 = f32[1024,128]{1,0:T(8,128)S(1)} fusion(s32[1024]{0:T(1024)S(1)} %bitcast.14, f32[1024,128]{1,0:T(8,128)S(1)} %get-tuple-element.108, bf16[8,1024,128]{2,1,0:T(8,128)(2,1)} %get-tuple-element.118, s32[]{:T(128)S(6)} %copy.7, pred[]{:T(512)S(6)} %compare.3), kind=kOutput, calls=%fused_computation.6.clone.1 | convolution fusion | flops 269746176 | bytes 1314821 | tf_op jit(solution)/shard_map/while/body/eval_jaxpr/nk,nd->kd/dot_general | solution.py:22
  10.6 0.5 convert_reduce_fusion.2
  11.1 2.5 %fusion.14 = f32[1024,128]{1,0:T(8,128)S(1)} fusion(s32[1024]{0:T(1024)S(1)} %bitcast.14, f32[1024,128]{1,0:T(8,128)S(1)} %get-tuple-element.108, bf16[8,1024,128]{2,1,0:T(8,128)(2,1)} %get-tuple-element.118, s32[]{:T(128)S(6)} %copy.7, pred[]{:T(512)S(6)} %compare.3), kind=kOutput, calls=%fused_computation.6.clone.1 | convolution fusion | flops 269746176 | bytes 1314821 | tf_op jit(solution)/shard_map/while/body/eval_jaxpr/nk,nd->kd/dot_general | solution.py:22
  13.6 0.5 convert_reduce_fusion.2
  14.2 2.5 %fusion.14 = f32[1024,128]{1,0:T(8,128)S(1)} fusion(s32[1024]{0:T(1024)S(1)} %bitcast.14, f32[1024,128]{1,0:T(8,128)S(1)} %get-tuple-element.108, bf16[8,1024,128]{2,1,0:T(8,128)(2,1)} %get-tuple-element.118, s32[]{:T(128)S(6)} %copy.7, pred[]{:T(512)S(6)} %compare.3), kind=kOutput, calls=%fused_computation.6.clone.1 | convolution fusion | flops 269746176 | bytes 1314821 | tf_op jit(solution)/shard_map/while/body/eval_jaxpr/nk,nd->kd/dot_general | solution.py:22
  16.7 0.5 convert_reduce_fusion.2
  17.2 2.5 %fusion.14 = f32[1024,128]{1,0:T(8,128)S(1)} fusion(s32[1024]{0:T(1024)S(1)} %bitcast.14, f32[1024,128]{1,0:T(8,128)S(1)} %get-tuple-element.108, bf16[8,1024,128]{2,1,0:T(8,128)(2,1)} %get-tuple-element.118, s32[]{:T(128)S(6)} %copy.7, pred[]{:T(512)S(6)} %compare.3), kind=kOutput, calls=%fused_computation.6.clone.1 | convolution fusion | flops 269746176 | bytes 1314821 | tf_op jit(solution)/shard_map/while/body/eval_jaxpr/nk,nd->kd/dot_general | solution.py:22
  19.7 0.5 convert_reduce_fusion.2
  20.3 2.5 %fusion.14 = f32[1024,128]{1,0:T(8,128)S(1)} fusion(s32[1024]{0:T(1024)S(1)} %bitcast.14, f32[1024,128]{1,0:T(8,128)S(1)} %get-tuple-element.108, bf16[8,1024,128]{2,1,0:T(8,128)(2,1)} %get-tuple-element.118, s32[]{:T(128)S(6)} %copy.7, pred[]{:T(512)S(6)} %compare.3), kind=kOutput, calls=%fused_computation.6.clone.1 | convolution fusion | flops 269746176 | bytes 1314821 | tf_op jit(solution)/shard_map/while/body/eval_jaxpr/nk,nd->kd/dot_general | solution.py:22
  22.8 0.5 convert_reduce_fusion.2
  23.3 2.5 %fusion.14 = f32[1024,128]{1,0:T(8,128)S(1)} fusion(s32[1024]{0:T(1024)S(1)} %bitcast.14, f32[1024,128]{1,0:T(8,128)S(1)} %get-tuple-element.108, bf16[8,1024,128]{2,1,0:T(8,128)(2,1)} %get-tuple-element.118, s32[]{:T(128)S(6)} %copy.7, pred[]{:T(512)S(6)} %compare.3), kind=kOutput, calls=%fused_computation.6.clone.1 | convolution fusion | flops 269746176 | bytes 1314821 | tf_op jit(solution)/shard_map/while/body/eval_jaxpr/nk,nd->kd/dot_general | solution.py:22
  25.9 0.5 convert_reduce_fusion.2
  26.4 2.5 %fusion.14 = f32[1024,128]{1,0:T(8,128)S(1)} fusion(s32[1024]{0:T(1024)S(1)} %bitcast.14, f32[1024,128]{1,0:T(8,128)S(1)} %get-tuple-element.108, bf16[8,1024,128]{2,1,0:T(8,128)(2,1)} %get-tuple-element.118, s32[]{:T(128)S(6)} %copy.7, pred[]{:T(512)S(6)} %compare.3), kind=kOutput, calls=%fused_computation.6.clone.1 | convolution fusion | flops 269746176 | bytes 1314821 | tf_op jit(solution)/shard_map/while/body/eval_jaxpr/nk,nd->kd/dot_general | solution.py:22
  28.9 0.5 convert_reduce_fusion.2
  29.5 2.5 %fusion.14 = f32[1024,128]{1,0:T(8,128)S(1)} fusion(s32[1024]{0:T(1024)S(1)} %bitcast.14, f32[1024,128]{1,0:T(8,128)S(1)} %get-tuple-element.108, bf16[8,1024,128]{2,1,0:T(8,128)(2,1)} %get-tuple-element.118, s32[]{:T(128)S(6)} %copy.7, pred[]{:T(512)S(6)} %compare.3), kind=kOutput, calls=%fused_computation.6.clone.1 | convolution fusion | flops 269746176 | bytes 1314821 | tf_op jit(solution)/shard_map/while/body/eval_jaxpr/nk,nd->kd/dot_general | solution.py:22
  32.0 0.5 convert_reduce_fusion.2
  32.5 0.0 copy-start.1
  32.5 0.0 copy-start
  32.5 0.8 copy-done.1
  33.3 0.0 all-reduce.2.cloned.1.call-update
  33.3 42.1 %psum.15 = f32[1024]{0:T(1024)S(1)} all-reduce(f32[1024]{0:T(1024)S(1)} %get-tuple-element.36), channel_id=1, replica_groups=mesh['grp'=4,'word'=8] {'grp','word'}, use_global_device_ids=true, to_apply=%region_4.5 | all-reduce | flops 1024 | bytes 8192 | tf_op jit(solution)/shard_map/psum | solution.py:37
  75.4 2.8 %multiply_reduce_fusion.1 = f32[8192]{0:T(1024)S(1)} fusion(bf16[8192,128]{1,0:T(8,128)(2,1)} %bitcast.12), kind=kLoop, calls=%fused_computation.13 | loop fusion | flops 3137536 | bytes 2129920 | tf_op jit(solution)/shard_map/reduce_sum | solution.py:34
  78.2 87.2 %all-reduce.2.cloned.1.call-done = f32[1024,128]{1,0:T(8,128)} async-done(((f32[1024,128]{1,0:T(8,128)}), f32[1024,128]{1,0:T(8,128)}) %all-reduce.2.cloned.1.call-update) | async-done | bytes 524304 | tf_op jit(solution)/shard_map/psum | solution.py:37
  165.4 1.4 multiply_reduce_fusion.2
  166.8 0.6 constant_dynamic-slice_fusion.1
  167.4 0.0 copy-done
  167.4 7.3 %multiply_reduce_fusion = f32[8192]{0:T(1024)} fusion(f32[1024]{0:T(1024)S(1)} %get-tuple-element.67, f32[8192]{0:T(1024)S(1)} %multiply_reduce_fusion.1, bf16[1024,128]{1,0:T(8,128)(2,1)S(1)} %get-tuple-element.68, bf16[8192,128]{1,0:T(8,128)(2,1)S(1)} %bitcast.13), kind=kOutput, calls=%fused_computation.12 | convolution fusion | flops 2189418496 | bytes 2428928 | tf_op jit(solution)/shard_map/dot_general | solution.py:41
  (18 shorter events, 0.1 us)
Async XLA Ops:
  7.2 158.2 %all-reduce.2.cloned.1.call-start = ((), (), s32[]{:S(2)}) async-start(), calls=%async_computation | async-start | bytes 1048576 | tf_op jit(solution)/shard_map/psum | solution.py:37
  32.5 0.8 copy-start.1
  32.5 134.9 %copy-start = (bf16[8,1024,128]{2,1,0:T(8,128)(2,1)S(1)}, bf16[8,1024,128]{2,1,0:T(8,128)(2,1)}, u32[]{:S(2)}) copy-start(bf16[8,1024,128]{2,1,0:T(8,128)(2,1)} %get-tuple-element.122) | copy-start | bytes 6291460
Sparse Core Ops, SparseCore 0:
  33.5 131.8 all-reduce.1
where the time goes:
time: 182 us
  waiting for transfers between devices  87.2 us (48%)
  blocking collectives  42.1 us (23%)
  matrix products  27.4 us (15%)
  between operations  14.1 us (8%)
  other arithmetic  8.02 us (4%)
  local copies, waits for them, and re-layouts  2.27 us (1%)
    psum x1, waiting for transfers between devices, on_device(): total, count = lax.psum((total, count), ('grp', 'word'))  87.2 us
    psum x1, blocking collectives, on_device(): total, count = lax.psum((total, count), ('grp', 'word'))  42.1 us
    dot_general x8, matrix products, step(): jnp.einsum('nk,nd->kd', onehot, xb, preferred_element_type=jnp.float32)  20.1 us
    dot_general x1, matrix products, on_device(): dots = jnp.dot(descriptors, whole.T, preferred_element_type=jnp.float32)  7.29 us
    reduce_sum x8, other arithmetic, step(): count = count + jnp.sum(onehot.astype(jnp.float32), axis=0)  3.82 us
  transfers between devices with their start and end apart: 1, of which 1 were waited for; matrix products, arithmetic and copies ran while one was open for 2% of the time, Pallas kernels for 0%

commit v1 on v0

v1 whole, which is shorter than its diff:
```python
import functools

import jax
import jax.numpy as jnp
from jax import lax
from jax.experimental import pallas as pl
from jax.experimental.pallas import tpu as pltpu
from jax.sharding import PartitionSpec as P

K = 1024
SPREAD = 64
HALF = SPREAD // 2
AUX = 8
BOTH = ("grp", "word")
F32 = jnp.float32
BF16 = jnp.bfloat16
NT = (((1,), (1,)), ((), ()))
VMEM = pl.BlockSpec(memory_space=pltpu.VMEM)
HBM = pl.BlockSpec(memory_space=pltpu.HBM)
SMALL = pltpu.CompilerParams(vmem_limit_bytes=16 << 20)


def split3(v):
    hi = v.astype(BF16)
    rest = v - hi.astype(F32)
    mid = rest.astype(BF16)
    low = (rest - mid.astype(F32)).astype(BF16)
    return hi, mid, low


def sums_kernel(ids_hbm, x_hbm, keep_ref, send_ref, ids_ref, x_ref, sem):
    core = lax.axis_index("word") % 2
    load_ids = pltpu.make_async_copy(ids_hbm, ids_ref, sem.at[0])
    load_ids.start()
    load = pltpu.make_async_copy(x_hbm, x_ref, sem.at[1])
    load.start()
    load_ids.wait()
    slot = lax.broadcasted_iota(jnp.int32, (SPREAD, 128), 0)
    ids = ids_ref[...]
    at = jnp.bitwise_and(ids, SPREAD - 1)
    total = jnp.zeros((SPREAD, 128), F32)
    pieces = []
    for r in range(ids.shape[0]):
        hit = jnp.where(slot == at[r : r + 1, :], 1.0, 0.0)
        total = total + hit
        pieces.append(hit.astype(BF16))
    first = ids[0:1, 0:1]
    rel = jnp.bitwise_and(ids - first + K // 2, K - 1)
    low = jnp.min(jnp.min(rel, axis=0, keepdims=True), axis=1, keepdims=True)
    start = jnp.bitwise_and(first + low - K // 2, K - 1)
    lane = lax.broadcasted_iota(jnp.int32, (AUX, 128), 1)
    own = jnp.bitwise_and(lane, SPREAD - 1)
    word = jnp.bitwise_and(start + jnp.bitwise_and(own - start, SPREAD - 1), K - 1)
    place = ((word // SPREAD) * HALF + jnp.bitwise_and(word, HALF - 1)).astype(F32)
    column = jnp.sum(total, axis=1, keepdims=True)
    wide = jnp.broadcast_to(column, (SPREAD, 128))
    row = jnp.concatenate([wide, wide], axis=0).T[0:AUX, :]
    aux0 = jnp.where(lane < HALF, place, pltpu.roll(row, HALF, 1))
    aux1 = jnp.where(lane < HALF, pltpu.roll(place, 128 - HALF, 1), row)
    aux0 = jnp.where(lane < SPREAD, aux0, 0.0)
    aux1 = jnp.where(lane < SPREAD, aux1, 0.0)
    keep_ref[HALF : HALF + AUX, :] = jnp.where(core == 0, aux0, aux1)
    send_ref[HALF : HALF + AUX, :] = pltpu.roll(jnp.where(core == 0, aux1, aux0), SPREAD, 1)
    load.wait()
    sums = jnp.dot(jnp.concatenate(pieces, axis=1), x_ref[...], preferred_element_type=F32)
    keep_ref[0:HALF, :] = jnp.where(core == 0, sums[0:HALF], sums[HALF:SPREAD])
    send_ref[0:HALF, :] = jnp.where(core == 0, sums[HALF:SPREAD], sums[0:HALF])


def window_sums(ids, x):
    rows, depth = x.shape
    out = jax.ShapeDtypeStruct((HALF + AUX, depth), F32)
    return pl.pallas_call(
        sums_kernel,
        in_specs=[HBM, HBM],
        out_specs=(VMEM, VMEM),
        out_shape=(out, out),
        scratch_shapes=[
            pltpu.VMEM((rows // 128, 128), jnp.int32),
            pltpu.VMEM((rows, depth), BF16),
            pltpu.SemaphoreType.DMA((2,)),
        ],
        compiler_params=SMALL,
        name="window_sums",
    )(pltpu.with_memory_space_constraint(ids, pltpu.HBM), pltpu.with_memory_space_constraint(x, pltpu.HBM))


def norms_kernel(x_ref, out_ref):
    n = x_ref.shape[0]
    xf = x_ref[...].astype(F32)
    sq = xf * xf
    hi = sq.astype(BF16)
    low = (sq - hi.astype(F32)).astype(BF16)
    both = jnp.concatenate([hi, low], axis=1)
    ones = jnp.ones((8, both.shape[1]), BF16)
    row = lax.dot_general(ones, both, NT, preferred_element_type=F32)
    for r in range(n // 128):
        out_ref[r : r + 1, :] = row[0:1, r * 128 : (r + 1) * 128]


def norms(x):
    rows, depth = x.shape
    chunk = min(2048, rows)
    return pl.pallas_call(
        norms_kernel,
        grid=(rows // chunk,),
        in_specs=[pl.BlockSpec((chunk, depth), lambda i: (i, 0))],
        out_specs=pl.BlockSpec((chunk // 128, 128), lambda i: (i, 0)),
        out_shape=jax.ShapeDtypeStruct((rows // 128, 128), F32),
        cost_estimate=pl.CostEstimate(flops=2 * rows * depth, bytes_accessed=2 * rows * depth, transcendentals=0),
        compiler_params=SMALL,
        name="norms",
    )(x)


def means_kernel(parts, *refs):
    ins, out_ref = refs[:parts], refs[parts]
    rows = ins[0].shape[0] - AUX
    half = out_ref.shape[0]
    target = lax.broadcasted_iota(jnp.int32, (half, 128), 0).astype(F32)
    pieces, values = [], []
    count = jnp.zeros((half, 128), F32)
    for ref in ins:
        for pair in range(rows // 128):
            a = ref[rows + 2 * pair : rows + 2 * pair + 1, :]
            b = ref[rows + 2 * pair + 1 : rows + 2 * pair + 2, :]
            lane = lax.broadcasted_iota(jnp.int32, (1, 128), 1)
            pa = jnp.where(lane < 32, a, pltpu.roll(a, 96, 1))
            ca = jnp.where(lane < 32, pltpu.roll(a, 96, 1), pltpu.roll(a, 64, 1))
            pb = jnp.where(lane < 96, pltpu.roll(b, 64, 1), pltpu.roll(b, 32, 1))
            cb = jnp.where(lane < 96, pltpu.roll(b, 32, 1), b)
            place = jnp.where(lane < 64, pa, pb)
            amount = jnp.where(lane < 64, ca, cb)
            hit = target == place
            count = count + jnp.where(hit, amount, 0.0)
            pieces.append(jnp.where(hit, 1.0, 0.0).astype(BF16))
            values.append(jnp.concatenate(split3(ref[128 * pair : 128 * pair + 128, :]), axis=1))
    onehot = jnp.concatenate(pieces, axis=1)
    table = jnp.concatenate(values, axis=0)
    wide = jnp.dot(onehot, table, preferred_element_type=F32)
    sums = wide[:, 0:128] + wide[:, 128:256] + wide[:, 256:384]
    out_ref[...] = (sums / jnp.sum(count, axis=1, keepdims=True)).astype(BF16)


def means(parts, half):
    depth = parts[0].shape[1]
    return pl.pallas_call(
        functools.partial(means_kernel, len(parts)),
        in_specs=[VMEM] * len(parts),
        out_specs=VMEM,
        compiler_params=SMALL,
        out_shape=jax.ShapeDtypeStruct((half, depth), BF16),
        name="means",
    )(*parts)


def nearest_kernel(last, cent_ref, x_ref, *refs):
    if last:
        near_ref, norm_ref, out_ref, table = refs
    else:
        out_ref, table = refs
    words, depth = cent_ref.shape
    n = x_ref.shape[0]

    cf = cent_ref[...].astype(F32)
    norm = jnp.broadcast_to(0.5 * jnp.sum(cf * cf, axis=1, keepdims=True), (words, depth))
    lane = lax.broadcasted_iota(jnp.int32, (words, depth), 1)
    hi, mid, low = [p.astype(F32) for p in split3(norm)]
    extra = jnp.where(lane == 0, hi, jnp.where(lane == 1, mid, jnp.where(lane == 2, low, 0.0)))
    table[:, 0:depth] = (-2.0 * cf).astype(BF16)
    table[:, depth : 2 * depth] = extra.astype(BF16)
    cols = 256
    twos = jnp.full((cols, depth), 2.0, BF16)
    for t in range(n // cols):
        full = jnp.concatenate([x_ref[t * cols : (t + 1) * cols, :], twos], axis=1)
        d = lax.dot_general(table[...], full, NT, preferred_element_type=F32)
        row = jnp.min(jnp.min(d.reshape(words // 8, 8, cols), axis=0), axis=0, keepdims=True)
        for r in range(cols // 128):
            at = t * (cols // 128) + r
            value = row[0:1, r * 128 : (r + 1) * 128]
            if last:
                value = jnp.minimum(value, near_ref[at : at + 1, :])
                value = (value + norm_ref[at : at + 1, :]) * (1.0 / depth)
            out_ref[at : at + 1, :] = value


def nearest(cent, x, near=None, norm=None):
    rows, depth = x.shape
    words = cent.shape[0]
    last = near is not None
    return pl.pallas_call(
        functools.partial(nearest_kernel, last),
        in_specs=[VMEM] * (4 if last else 2),
        out_specs=VMEM,
        out_shape=jax.ShapeDtypeStruct((rows // 128, 128), F32),
        scratch_shapes=[pltpu.VMEM((words, 2 * depth), BF16)],
        cost_estimate=pl.CostEstimate(flops=4 * rows * depth * words, bytes_accessed=2 * rows * depth, transcendentals=0),
        compiler_params=SMALL,
        name="nearest_last" if last else "nearest_first",
    )(*((cent, x, near, norm) if last else (cent, x)))


def moved(a, axis, size, flip):
    return lax.ppermute(a, axis, [(i, i ^ flip) for i in range(size)])


def gathered(groups, words, descriptors, word_ids):
    rows, depth = descriptors.shape
    ids = word_ids.reshape(rows // 128, 128)
    keep, send = window_sums(ids, descriptors)
    got = moved(send, "word", words, 1)
    mine = jnp.concatenate([keep[:HALF], got[:HALF], keep[HALF:] + got[HALF:]], axis=0)
    line = [mine] + [moved(mine, "word", words, 2 * k) for k in range(1, words // 2)]
    aux = [a[SPREAD : SPREAD + 1] for a in line]
    aux.append(jnp.zeros((-len(line) % AUX, depth), F32))
    block = jnp.concatenate([a[:SPREAD] for a in line] + aux, axis=0)
    blocks = [block] + [moved(block, "grp", groups, k) for k in range(1, groups)]
    xnorm = norms(descriptors)
    half = means(blocks, K // 2)
    other = moved(half, "word", words, 1)
    near = nearest(half, descriptors)
    near = nearest(other, descriptors, near, xnorm)
    index = lax.axis_index("word")
    owned = K // words
    cut = [lax.dynamic_slice_in_dim(h, index * (owned // 2), owned // 2, 0) for h in (half, other)]
    cut = [c.reshape(owned // SPREAD, 1, HALF, depth) for c in cut]
    even = index % 2 == 0
    cent = jnp.concatenate([jnp.where(even, cut[0], cut[1]), jnp.where(even, cut[1], cut[0])], axis=1)
    return cent.reshape(owned, depth), near.reshape(rows)


def summed(words, descriptors, word_ids):
    rows, depth = descriptors.shape
    keep, send = window_sums(word_ids.reshape(rows // 128, 128), descriptors)
    index = lax.axis_index("word")
    even = index % 2 == 0
    near_half = jnp.where(even, keep, send)
    far_half = jnp.where(even, send, keep)
    target = lax.broadcasted_iota(jnp.int32, (K // 2, HALF), 0)
    totals, counts = [], []
    for part in (near_half, far_half):
        aux = part[HALF, :SPREAD] + part[HALF, SPREAD:]
        hit = target == aux[None, :HALF].astype(jnp.int32)
        counts.append(jnp.sum(jnp.where(hit, aux[None, HALF:], 0.0), axis=1))
        totals.append(jnp.dot(hit.astype(F32), part[:HALF], precision=lax.Precision.HIGHEST))
    total, count = lax.psum((jnp.concatenate(totals), jnp.concatenate(counts)), BOTH)
    cent = (total / count[:, None]).astype(BF16)
    near = nearest(cent[: K // 2], descriptors)
    near = nearest(cent[K // 2 :], descriptors, near, norms(descriptors))
    cent = cent.reshape(2, K // SPREAD, HALF, depth).swapaxes(0, 1).reshape(K, depth)
    owned = K // words
    return lax.dynamic_slice_in_dim(cent, index * owned, owned, 0), near.reshape(rows)


def solution(mesh):
    groups, words = mesh.shape["grp"], mesh.shape["word"]
    small = groups * words * SPREAD <= 2 * K and K // words >= SPREAD
    return jax.shard_map(
        functools.partial(gathered, groups, words) if small else functools.partial(summed, words),
        mesh=mesh,
        in_specs=(P(BOTH, None), P(BOTH)),
        out_specs=(P("word", None), P(BOTH)),
        check_vma=False,
    )
```

time: 182 us -> 32.1 us (0.18)
  waiting for transfers between devices: 87.2 us -> 10.5 us
  blocking collectives: 42.1 us -> 0 us
  matrix products: 27.4 us -> 0 us
  between operations: 14.1 us -> 0.73 us
  Pallas kernels: 0 us -> 10.2 us
  starting transfers between devices: 0.04 us -> 9.74 us
  other arithmetic: 8.02 us -> 0.04 us
    psum x1 -> x0, waiting for transfers between devices: 87.2 us -> none  [on_device(): total, count = lax.psum((total, count), ('grp', 'word'))]
    psum x1 -> x0, blocking collectives: 42.1 us -> none  [on_device(): total, count = lax.psum((total, count), ('grp', 'word'))]
    dot_general x9 -> x0, matrix products: 27.4 us -> none  [the longest x8 20.1 us: step(): jnp.einsum('nk,nd->kd', onehot, xb, preferred_element_type=jnp.float32)]
    ppermute x0 -> x8, waiting for transfers between devices: none -> 10.5 us  [moved(): return lax.ppermute(a, axis, [(i, i ^ flip) for i in range(size)])]
    pallas_call x0 -> x5, Pallas kernels: none -> 10.2 us  [the longest x2 5.51 us: nearest(): pl.pallas_call(functools.partial(nearest_kernel, last), in_specs=[VMEM] *...]
    ppermute x0 -> x8, starting transfers between devices: none -> 9.74 us  [moved(): return lax.ppermute(a, axis, [(i, i ^ flip) for i in range(size)])]
    reduce_sum x10 -> x0, other arithmetic: 7.97 us -> none  [the longest x8 3.82 us: step(): count = count + jnp.sum(onehot.astype(jnp.float32), axis=0)]
  transfers between devices with their start and end apart: 1 -> 8, of which waited for: 1 -> 6; matrix products, arithmetic and copies ran while one was open for 2% -> 0% of each run, Pallas kernels for 0% -> 13%
where the time goes in v1:
time: 32.1 us; the launch traced here: 31.9 us
  waiting for transfers between devices  10.5 us (33%)
  Pallas kernels  10.2 us (32%)
  starting transfers between devices  9.74 us (30%)
  between operations  0.73 us (2%)
  local copies, waits for them, and re-layouts  0.68 us (2%)
    ppermute x8, waiting for transfers between devices, moved(): return lax.ppermute(a, axis, [(i, i ^ flip) for i in range(size)])  10.5 us
    ppermute x8, starting transfers between devices, moved(): return lax.ppermute(a, axis, [(i, i ^ flip) for i in range(size)])  9.74 us
    pallas_call x2, Pallas kernels, nearest(): pl.pallas_call(functools.partial(nearest_kernel, last), in_specs=[VMEM] *...  5.51 us
    pallas_call x1, Pallas kernels, window_sums(): pl.pallas_call(sums_kernel, in_specs=[HBM, HBM], out_specs=(VMEM, VMEM),...  2.24 us
    pallas_call x1, Pallas kernels, norms(): pl.pallas_call(norms_kernel, grid=(rows // chunk,), in_specs=[pl.BlockSpe...  1.56 us
    pallas_call x1, Pallas kernels, means(): pl.pallas_call(functools.partial(means_kernel, len(parts)), in_specs=[VME...  0.9 us
  transfers between devices with their start and end apart: 8, of which 6 were waited for; matrix products, arithmetic and copies ran while one was open for 0% of the time, Pallas kernels for 13%

profile of v1, /device:TPU:0, one launch (start us, length us, event | category | flops | bytes accessed | tf_op | source)
XLA Modules:
  0.0 31.9 jit_solution(17260664939155564124)
XLA Ops:
  0.6 0.0 copy-start
  0.6 2.2 %window_sums.1 = (f32[40,128]{1,0:T(8,128)S(1)}, f32[40,128]{1,0:T(8,128)S(1)}) custom-call(s32[64,128]{1,0:T(8,128)} %bitcast.7, bf16[8192,128]{1,0:T(8,128)(2,1)} %x_ref.5), custom_call_target="tpu_custom_call" | custom-call | tf_op jit(solution)/shard_map/window_sums/pallas_call | solution.py:73
  2.9 0.6 %collective-permute-start = (f32[40,128]{1,0:T(8,128)S(1)}, f32[40,128]{1,0:T(8,128)S(1)}, u32[]{:S(2)}, u32[]{:S(2)}) collective-permute-start(f32[40,128]{1,0:T(8,128)S(1)} %get-tuple-element.5), channel_id=1, source_target_pairs={{0,1},{1,0},{2,3},{3,2},{4,5},{5,4},{6,7},{7,6},{8,9},{9,8},{10,11... | collective-permute-start | bytes 61448 | tf_op jit(solution)/shard_map/ppermute | solution.py:204
  3.4 0.8 %collective-permute-done = f32[40,128]{1,0:T(8,128)S(1)} collective-permute-done((f32[40,128]{1,0:T(8,128)S(1)}, f32[40,128]{1,0:T(8,128)S(1)}, u32[]{:S(2)}, u32[]{:S(2)}) %collective-permute-start) | collective-permute-done | bytes 20512 | tf_op jit(solution)/shard_map/ppermute | solution.py:204
  4.3 3.0 %collective-permute-start.1 = (f32[72,128]{1,0:T(8,128)S(1)}, f32[72,128]{1,0:T(8,128)S(1)}, u32[]{:S(2)}, u32[]{:S(2)}) collective-permute-start(f32[72,128]{1,0:T(8,128)S(1)} %pad_maximum_fusion), channel_id=1, source_target_pairs={{0,2},{1,3},{2,0},{3,1},{4,6},{5,7},{6,4},{7,5},{8,10},{9,11},{10,... | collective-permute-start | bytes 110600 | tf_op jit(solution)/shard_map/ppermute | solution.py:204
  7.3 2.6 %collective-permute-start.2 = (f32[72,128]{1,0:T(8,128)S(1)}, f32[72,128]{1,0:T(8,128)S(1)}, u32[]{:S(2)}, u32[]{:S(2)}) collective-permute-start(f32[72,128]{1,0:T(8,128)S(1)} %pad_maximum_fusion), channel_id=1, source_target_pairs={{0,4},{1,5},{2,6},{3,7},{4,0},{5,1},{6,2},{7,3},{8,12},{9,13},{10,... | collective-permute-start | bytes 110600 | tf_op jit(solution)/shard_map/ppermute | solution.py:204
  9.9 0.0 collective-permute-start.3
  9.9 0.0 collective-permute-done.1
  9.9 3.0 %collective-permute-done.2 = f32[72,128]{1,0:T(8,128)S(1)} collective-permute-done((f32[72,128]{1,0:T(8,128)S(1)}, f32[72,128]{1,0:T(8,128)S(1)}, u32[]{:S(2)}, u32[]{:S(2)}) %collective-permute-start.2) | collective-permute-done | bytes 36896 | tf_op jit(solution)/shard_map/ppermute | solution.py:204
  12.9 2.8 %collective-permute-done.3 = f32[72,128]{1,0:T(8,128)S(1)} collective-permute-done((f32[72,128]{1,0:T(8,128)S(1)}, f32[72,128]{1,0:T(8,128)S(1)}, u32[]{:S(2)}, u32[]{:S(2)}) %collective-permute-start.3) | collective-permute-done | bytes 36896 | tf_op jit(solution)/shard_map/ppermute | solution.py:204
  15.7 1.6 %collective-permute-start.4 = (f32[264,128]{1,0:T(8,128)S(1)}, f32[264,128]{1,0:T(8,128)S(1)}, u32[]{:S(2)}, u32[]{:S(2)}) collective-permute-start(f32[264,128]{1,0:T(8,128)S(1)} %concatenate.12.refs_0_), channel_id=1, source_target_pairs={{0,8},{8,0},{16,24},{24,16},{1,9},{9,1},{17,25},{25,17},{2,10},{10... | collective-permute-start | bytes 405512 | tf_op jit(solution)/shard_map/ppermute | solution.py:204
  17.2 1.5 %collective-permute-start.5 = (f32[264,128]{1,0:T(8,128)S(1)}, f32[264,128]{1,0:T(8,128)S(1)}, u32[]{:S(2)}, u32[]{:S(2)}) collective-permute-start(f32[264,128]{1,0:T(8,128)S(1)} %concatenate.12.refs_0_), channel_id=1, source_target_pairs={{0,16},{8,24},{16,0},{24,8},{1,17},{9,25},{17,1},{25,9},{2,18},{10... | collective-permute-start | bytes 405512 | tf_op jit(solution)/shard_map/ppermute | solution.py:204
  18.7 0.5 %collective-permute-start.6 = (f32[264,128]{1,0:T(8,128)S(1)}, f32[264,128]{1,0:T(8,128)S(1)}, u32[]{:S(2)}, u32[]{:S(2)}) collective-permute-start(f32[264,128]{1,0:T(8,128)S(1)} %concatenate.12.refs_0_), channel_id=1, source_target_pairs={{0,24},{8,16},{16,8},{24,0},{1,25},{9,17},{17,9},{25,1},{2,26},{10... | collective-permute-start | bytes 405512 | tf_op jit(solution)/shard_map/ppermute | solution.py:204
  19.2 0.0 copy-done
  19.2 1.6 %norms.1.refs_1_ = f32[64,128]{1,0:T(8,128)S(1)} custom-call(bf16[8192,128]{1,0:T(8,128)(2,1)S(1)} %copy-done), custom_call_target="tpu_custom_call" | custom-call | flops 2097152 | bytes 2097152 | tf_op jit(solution)/shard_map/norms/pallas_call | solution.py:104
  20.8 1.3 %collective-permute-done.4.refs_1_ = f32[264,128]{1,0:T(8,128)S(1)} collective-permute-done((f32[264,128]{1,0:T(8,128)S(1)}, f32[264,128]{1,0:T(8,128)S(1)}, u32[]{:S(2)}, u32[]{:S(2)}) %collective-permute-start.4) | collective-permute-done | bytes 135200 | tf_op jit(solution)/shard_map/ppermute | solution.py:204
  22.1 1.2 %collective-permute-done.5.refs_2_ = f32[264,128]{1,0:T(8,128)S(1)} collective-permute-done((f32[264,128]{1,0:T(8,128)S(1)}, f32[264,128]{1,0:T(8,128)S(1)}, u32[]{:S(2)}, u32[]{:S(2)}) %collective-permute-start.5) | collective-permute-done | bytes 135200 | tf_op jit(solution)/shard_map/ppermute | solution.py:204
  23.3 1.4 %collective-permute-done.6.refs_3_ = f32[264,128]{1,0:T(8,128)S(1)} collective-permute-done((f32[264,128]{1,0:T(8,128)S(1)}, f32[264,128]{1,0:T(8,128)S(1)}, u32[]{:S(2)}, u32[]{:S(2)}) %collective-permute-start.6) | collective-permute-done | bytes 135200 | tf_op jit(solution)/shard_map/ppermute | solution.py:204
  24.7 0.9 %means.1.cent_ref = bf16[512,128]{1,0:T(8,128)(2,1)S(1)} custom-call(f32[264,128]{1,0:T(8,128)S(1)} %concatenate.12.refs_0_, f32[264,128]{1,0:T(8,128)S(1)} %collective-permute-done.4.refs_1_, f32[264,128]{1,0:T(8,128)S(1)} %collective-permute-done.5.refs_2_, f32[264,128]{1,0:T(8,128)S(1)} %collective-permute-done.6.refs_3_), custom_call_target="tpu_custom_call" | custom-call | tf_op jit(solution)/shard_map/means/pallas_call | solution.py:147
  25.6 0.1 collective-permute-start.7
  25.7 2.5 %nearest_first.1.refs_0_ = f32[64,128]{1,0:T(8,128)S(1)} custom-call(bf16[512,128]{1,0:T(8,128)(2,1)S(1)} %means.1.cent_ref, bf16[8192,128]{1,0:T(8,128)(2,1)S(1)} %copy-done), custom_call_target="tpu_custom_call" | custom-call | flops 2147483648 | bytes 2097152 | tf_op jit(solution)/shard_map/nearest_first/pallas_call | solution.py:191
  28.2 0.0 collective-permute-done.7.cent_ref
  28.2 0.6 %copy.4 = bf16[2,2,32,128]{3,2,1,0:T(8,128)(2,1)} copy(bf16[2,2,32,128]{3,2,0,1:T(8,128)(2,1)S(1)} %pad_maximum_fusion.1) | data formatting | bytes 65536 | tf_op jit(solution)/shard_map/concatenate | solution.py:228
  28.9 3.1 %nearest_last.1 = f32[64,128]{1,0:T(8,128)} custom-call(bf16[512,128]{1,0:T(8,128)(2,1)S(1)} %collective-permute-done.7.cent_ref, bf16[8192,128]{1,0:T(8,128)(2,1)S(1)} %copy-done, f32[64,128]{1,0:T(8,128)S(1)} %nearest_first.1.refs_0_, f32[64,128]{1,0:T(8,128)S(1)} %norms.1.refs_1_), custom_call_target="tpu_custom_call" | custom-call | flops 2147483648 | bytes 2097152 | tf_op jit(solution)/shard_map/nearest_last/pallas_call | solution.py:191
  (15 shorter events, 0.1 us)
Async XLA Ops:
  0.6 18.6 %copy-start = (bf16[8192,128]{1,0:T(8,128)(2,1)S(1)}, bf16[8192,128]{1,0:T(8,128)(2,1)}, u32[]{:S(2)}) copy-start(bf16[8192,128]{1,0:T(8,128)(2,1)} %x_ref.5) | copy-start | bytes 6291460
  2.9 1.4 %collective-permute-start = (f32[40,128]{1,0:T(8,128)S(1)}, f32[40,128]{1,0:T(8,128)S(1)}, u32[]{:S(2)}, u32[]{:S(2)}) collective-permute-start(f32[40,128]{1,0:T(8,128)S(1)} %get-tuple-element.5), channel_id=1, source_target_pairs={{0,1},{1,0},{2,3},{3,2},{4,5},{5,4},{6,7},{7,6},{8,9},{9,8},{10,11... | collective-permute-start | bytes 61448 | tf_op jit(solution)/shard_map/ppermute | solution.py:204
  4.3 5.6 %collective-permute-start.1 = (f32[72,128]{1,0:T(8,128)S(1)}, f32[72,128]{1,0:T(8,128)S(1)}, u32[]{:S(2)}, u32[]{:S(2)}) collective-permute-start(f32[72,128]{1,0:T(8,128)S(1)} %pad_maximum_fusion), channel_id=1, source_target_pairs={{0,2},{1,3},{2,0},{3,1},{4,6},{5,7},{6,4},{7,5},{8,10},{9,11},{10,... | collective-permute-start | bytes 110600 | tf_op jit(solution)/shard_map/ppermute | solution.py:204
  7.3 5.6 %collective-permute-start.2 = (f32[72,128]{1,0:T(8,128)S(1)}, f32[72,128]{1,0:T(8,128)S(1)}, u32[]{:S(2)}, u32[]{:S(2)}) collective-permute-start(f32[72,128]{1,0:T(8,128)S(1)} %pad_maximum_fusion), channel_id=1, source_target_pairs={{0,4},{1,5},{2,6},{3,7},{4,0},{5,1},{6,2},{7,3},{8,12},{9,13},{10,... | collective-permute-start | bytes 110600 | tf_op jit(solution)/shard_map/ppermute | solution.py:204
  9.9 5.8 %collective-permute-start.3 = (f32[72,128]{1,0:T(8,128)S(1)}, f32[72,128]{1,0:T(8,128)S(1)}, u32[]{:S(2)}, u32[]{:S(2)}) collective-permute-start(f32[72,128]{1,0:T(8,128)S(1)} %pad_maximum_fusion), channel_id=1, source_target_pairs={{0,6},{1,7},{2,4},{3,5},{4,2},{5,3},{6,0},{7,1},{8,14},{9,15},{10,... | collective-permute-start | bytes 110600 | tf_op jit(solution)/shard_map/ppermute | solution.py:204
  15.7 6.4 %collective-permute-start.4 = (f32[264,128]{1,0:T(8,128)S(1)}, f32[264,128]{1,0:T(8,128)S(1)}, u32[]{:S(2)}, u32[]{:S(2)}) collective-permute-start(f32[264,128]{1,0:T(8,128)S(1)} %concatenate.12.refs_0_), channel_id=1, source_target_pairs={{0,8},{8,0},{16,24},{24,16},{1,9},{9,1},{17,25},{25,17},{2,10},{10... | collective-permute-start | bytes 405512 | tf_op jit(solution)/shard_map/ppermute | solution.py:204
  17.2 6.1 %collective-permute-start.5 = (f32[264,128]{1,0:T(8,128)S(1)}, f32[264,128]{1,0:T(8,128)S(1)}, u32[]{:S(2)}, u32[]{:S(2)}) collective-permute-start(f32[264,128]{1,0:T(8,128)S(1)} %concatenate.12.refs_0_), channel_id=1, source_target_pairs={{0,16},{8,24},{16,0},{24,8},{1,17},{9,25},{17,1},{25,9},{2,18},{10... | collective-permute-start | bytes 405512 | tf_op jit(solution)/shard_map/ppermute | solution.py:204
  18.7 6.0 %collective-permute-start.6 = (f32[264,128]{1,0:T(8,128)S(1)}, f32[264,128]{1,0:T(8,128)S(1)}, u32[]{:S(2)}, u32[]{:S(2)}) collective-permute-start(f32[264,128]{1,0:T(8,128)S(1)} %concatenate.12.refs_0_), channel_id=1, source_target_pairs={{0,24},{8,16},{16,8},{24,0},{1,25},{9,17},{17,9},{25,1},{2,26},{10... | collective-permute-start | bytes 405512 | tf_op jit(solution)/shard_map/ppermute | solution.py:204
  25.6 2.5 %collective-permute-start.7 = (bf16[512,128]{1,0:T(8,128)(2,1)S(1)}, bf16[512,128]{1,0:T(8,128)(2,1)S(1)}, u32[]{:S(2)}, u32[]{:S(2)}) collective-permute-start(bf16[512,128]{1,0:T(8,128)(2,1)S(1)} %means.1.cent_ref), channel_id=1, source_target_pairs={{0,1},{1,0},{2,3},{3,2},{4,5},{5,4},{6,7},{7,6},{8,9},{9,8},{10,11... | collective-permute-start | bytes 393224 | tf_op jit(solution)/shard_map/ppermute | solution.py:204

commit v2 on v1

--- a/solution.py
+++ b/solution.py
@@ -28,7 +28,7 @@
     return hi, mid, low
 
 
-def sums_kernel(ids_hbm, x_hbm, keep_ref, send_ref, ids_ref, x_ref, sem):
+def sums_kernel(ids_hbm, x_hbm, keep_ref, send_ref, x_ref, ids_ref, sem):
     core = lax.axis_index("word") % 2
     load_ids = pltpu.make_async_copy(ids_hbm, ids_ref, sem.at[0])
     load_ids.start()
@@ -73,13 +73,9 @@
     return pl.pallas_call(
         sums_kernel,
         in_specs=[HBM, HBM],
-        out_specs=(VMEM, VMEM),
-        out_shape=(out, out),
-        scratch_shapes=[
-            pltpu.VMEM((rows // 128, 128), jnp.int32),
-            pltpu.VMEM((rows, depth), BF16),
-            pltpu.SemaphoreType.DMA((2,)),
-        ],
+        out_specs=(VMEM, VMEM, VMEM),
+        out_shape=(out, out, jax.ShapeDtypeStruct(x.shape, x.dtype)),
+        scratch_shapes=[pltpu.VMEM((rows // 128, 128), jnp.int32), pltpu.SemaphoreType.DMA((2,))],
         compiler_params=SMALL,
         name="window_sums",
     )(pltpu.with_memory_space_constraint(ids, pltpu.HBM), pltpu.with_memory_space_constraint(x, pltpu.HBM))
@@ -154,9 +150,21 @@
     )(*parts)
 
 
+def own_words(mine_ref, other_ref, own_ref):
+    index = lax.axis_index("word")
+    even = index % 2 == 0
+    blocks = own_ref.shape[0] // SPREAD
+    for b in range(blocks):
+        rows = pl.ds(pl.multiple_of((index * blocks + b) * HALF, HALF), HALF)
+        mine, other = mine_ref[rows, :], other_ref[rows, :]
+        own_ref[b * SPREAD : b * SPREAD + HALF, :] = jnp.where(even, mine, other)
+        own_ref[b * SPREAD + HALF : (b + 1) * SPREAD, :] = jnp.where(even, other, mine)
+
+
 def nearest_kernel(last, cent_ref, x_ref, *refs):
     if last:
-        near_ref, norm_ref, out_ref, table = refs
+        mine_ref, near_ref, norm_ref, own_ref, out_ref, table = refs
+        own_words(mine_ref, cent_ref, own_ref)
     else:
         out_ref, table = refs
     words, depth = cent_ref.shape
@@ -184,54 +192,53 @@
             out_ref[at : at + 1, :] = value
 
 
-def nearest(cent, x, near=None, norm=None):
+def nearest(cent, x, *last, owned=0):
     rows, depth = x.shape
     words = cent.shape[0]
-    last = near is not None
-    return pl.pallas_call(
-        functools.partial(nearest_kernel, last),
-        in_specs=[VMEM] * (4 if last else 2),
-        out_specs=VMEM,
-        out_shape=jax.ShapeDtypeStruct((rows // 128, 128), F32),
+    out = jax.ShapeDtypeStruct((rows // 128, 128), F32)
+    own = jax.ShapeDtypeStruct((owned, depth), BF16)
+    return pl.pallas_call(
+        functools.partial(nearest_kernel, bool(last)),
+        in_specs=[VMEM] * (2 + len(last)),
+        out_specs=(VMEM, VMEM) if last else VMEM,
+        out_shape=(own, out) if last else out,
         scratch_shapes=[pltpu.VMEM((words, 2 * depth), BF16)],
         cost_estimate=pl.CostEstimate(flops=4 * rows * depth * words, bytes_accessed=2 * rows * depth, transcendentals=0),
         compiler_params=SMALL,
         name="nearest_last" if last else "nearest_first",
-    )(*((cent, x, near, norm) if last else (cent, x)))
+    )(cent, x, *last)
 
 
 def moved(a, axis, size, flip):
     return lax.ppermute(a, axis, [(i, i ^ flip) for i in range(size)])
+
+
+def far_first(size):
+    return list(range(size // 2, size)) + list(range(1, size // 2))
 
 
 def gathered(groups, words, descriptors, word_ids):
     rows, depth = descriptors.shape
     ids = word_ids.reshape(rows // 128, 128)
-    keep, send = window_sums(ids, descriptors)
+    keep, send, x = window_sums(ids, descriptors)
     got = moved(send, "word", words, 1)
     mine = jnp.concatenate([keep[:HALF], got[:HALF], keep[HALF:] + got[HALF:]], axis=0)
-    line = [mine] + [moved(mine, "word", words, 2 * k) for k in range(1, words // 2)]
+    line = [mine] + [moved(mine, "word", words, 2 * k) for k in far_first(words // 2)]
     aux = [a[SPREAD : SPREAD + 1] for a in line]
     aux.append(jnp.zeros((-len(line) % AUX, depth), F32))
     block = jnp.concatenate([a[:SPREAD] for a in line] + aux, axis=0)
-    blocks = [block] + [moved(block, "grp", groups, k) for k in range(1, groups)]
-    xnorm = norms(descriptors)
+    blocks = [block] + [moved(block, "grp", groups, k) for k in range(groups - 1, 0, -1)]
+    xnorm = norms(x)
     half = means(blocks, K // 2)
     other = moved(half, "word", words, 1)
-    near = nearest(half, descriptors)
-    near = nearest(other, descriptors, near, xnorm)
-    index = lax.axis_index("word")
-    owned = K // words
-    cut = [lax.dynamic_slice_in_dim(h, index * (owned // 2), owned // 2, 0) for h in (half, other)]
-    cut = [c.reshape(owned // SPREAD, 1, HALF, depth) for c in cut]
-    even = index % 2 == 0
-    cent = jnp.concatenate([jnp.where(even, cut[0], cut[1]), jnp.where(even, cut[1], cut[0])], axis=1)
-    return cent.reshape(owned, depth), near.reshape(rows)
+    near = nearest(half, x)
+    cent, near = nearest(other, x, half, near, xnorm, owned=K // words)
+    return cent, near.reshape(rows)
 
 
 def summed(words, descriptors, word_ids):
     rows, depth = descriptors.shape
-    keep, send = window_sums(word_ids.reshape(rows // 128, 128), descriptors)
+    keep, send, x = window_sums(word_ids.reshape(rows // 128, 128), descriptors)
     index = lax.axis_index("word")
     even = index % 2 == 0
     near_half = jnp.where(even, keep, send)
@@ -245,8 +252,8 @@
         totals.append(jnp.dot(hit.astype(F32), part[:HALF], precision=lax.Precision.HIGHEST))
     total, count = lax.psum((jnp.concatenate(totals), jnp.concatenate(counts)), BOTH)
     cent = (total / count[:, None]).astype(BF16)
-    near = nearest(cent[: K // 2], descriptors)
-    near = nearest(cent[K // 2 :], descriptors, near, norms(descriptors))
+    near = nearest(cent[: K // 2], x)
+    unused, near = nearest(cent[K // 2 :], x, cent[: K // 2], near, norms(x), owned=SPREAD)
     cent = cent.reshape(2, K // SPREAD, HALF, depth).swapaxes(0, 1).reshape(K, depth)
     owned = K // words
     return lax.dynamic_slice_in_dim(cent, index * owned, owned, 0), near.reshape(rows)

time: 32.1 us -> 28.8 us (0.90)
  waiting for transfers between devices: 10.5 us -> 8.05 us
  local copies, waits for them, and re-layouts: 0.68 us -> 0.06 us
    ppermute x8, waiting for transfers between devices: 10.5 us -> 8.05 us  [moved(): return lax.ppermute(a, axis, [(i, i ^ flip) for i in range(size)])]
    concatenate x1 -> x0, local copies, waits for them, and re-layouts: 0.62 us -> none  [gathered(): jnp.concatenate([jnp.where(even, cut[0], cut[1]), jnp.where(even, cut[1],...]
  transfers between devices with their start and end apart: 8 -> 8, of which waited for: 6 -> 6; matrix products, arithmetic and copies ran while one was open for 0% -> 0% of each run, Pallas kernels for 13% -> 14%
where the time goes in v2:
time: 28.8 us; the launch traced here: 28.6 us
  Pallas kernels  10.1 us (35%)
  starting transfers between devices  9.74 us (34%)
  waiting for transfers between devices  8.05 us (28%)
  between operations  0.71 us (2%)
    ppermute x8, starting transfers between devices, moved(): return lax.ppermute(a, axis, [(i, i ^ flip) for i in range(size)])  9.74 us
    ppermute x8, waiting for transfers between devices, moved(): return lax.ppermute(a, axis, [(i, i ^ flip) for i in range(size)])  8.05 us
    pallas_call x2, Pallas kernels, nearest(): pl.pallas_call(functools.partial(nearest_kernel, bool(last)), in_specs=[V...  5.5 us
    pallas_call x1, Pallas kernels, window_sums(): pl.pallas_call(sums_kernel, in_specs=[HBM, HBM], out_specs=(VMEM, VMEM, V...  2.09 us
    pallas_call x1, Pallas kernels, norms(): pl.pallas_call(norms_kernel, grid=(rows // chunk,), in_specs=[pl.BlockSpe...  1.56 us
    pallas_call x1, Pallas kernels, means(): pl.pallas_call(functools.partial(means_kernel, len(parts)), in_specs=[VME...  0.9 us
  transfers between devices with their start and end apart: 8, of which 6 were waited for; matrix products, arithmetic and copies ran while one was open for 0% of the time, Pallas kernels for 14%

profile of v2, /device:TPU:0, one launch (start us, length us, event | category | flops | bytes accessed | tf_op | source)
XLA Modules:
  0.0 28.6 jit_solution(2925200727171805516)
XLA Ops:
  0.6 2.1 %window_sums.1 = (f32[40,128]{1,0:T(8,128)S(1)}, f32[40,128]{1,0:T(8,128)S(1)}, bf16[8192,128]{1,0:T(8,128)(2,1)S(1)}) custom-call(s32[64,128]{1,0:T(8,128)} %bitcast.2, bf16[8192,128]{1,0:T(8,128)(2,1)} %x_hbm.1), custom_call_target="tpu_custom_call" | custom-call | tf_op jit(solution)/shard_map/window_sums/pallas_call | solution.py:73
  2.7 0.6 %collective-permute-start = (f32[40,128]{1,0:T(8,128)S(1)}, f32[40,128]{1,0:T(8,128)S(1)}, u32[]{:S(2)}, u32[]{:S(2)}) collective-permute-start(f32[40,128]{1,0:T(8,128)S(1)} %get-tuple-element.8), channel_id=1, source_target_pairs={{0,1},{1,0},{2,3},{3,2},{4,5},{5,4},{6,7},{7,6},{8,9},{9,8},{10,11... | collective-permute-start | bytes 61448 | tf_op jit(solution)/shard_map/ppermute | solution.py:213
  3.3 0.8 %collective-permute-done = f32[40,128]{1,0:T(8,128)S(1)} collective-permute-done((f32[40,128]{1,0:T(8,128)S(1)}, f32[40,128]{1,0:T(8,128)S(1)}, u32[]{:S(2)}, u32[]{:S(2)}) %collective-permute-start) | collective-permute-done | bytes 20512 | tf_op jit(solution)/shard_map/ppermute | solution.py:213
  4.1 4.0 %collective-permute-start.1 = (f32[72,128]{1,0:T(8,128)S(1)}, f32[72,128]{1,0:T(8,128)S(1)}, u32[]{:S(2)}, u32[]{:S(2)}) collective-permute-start(f32[72,128]{1,0:T(8,128)S(1)} %pad_maximum_fusion), channel_id=1, source_target_pairs={{0,4},{1,5},{2,6},{3,7},{4,0},{5,1},{6,2},{7,3},{8,12},{9,13},{10,... | collective-permute-start | bytes 110600 | tf_op jit(solution)/shard_map/ppermute | solution.py:213
  8.1 1.3 %collective-permute-start.2 = (f32[72,128]{1,0:T(8,128)S(1)}, f32[72,128]{1,0:T(8,128)S(1)}, u32[]{:S(2)}, u32[]{:S(2)}) collective-permute-start(f32[72,128]{1,0:T(8,128)S(1)} %pad_maximum_fusion), channel_id=1, source_target_pairs={{0,6},{1,7},{2,4},{3,5},{4,2},{5,3},{6,0},{7,1},{8,14},{9,15},{10,... | collective-permute-start | bytes 110600 | tf_op jit(solution)/shard_map/ppermute | solution.py:213
  9.5 0.2 collective-permute-start.3
  9.7 0.4 %collective-permute-done.1 = f32[72,128]{1,0:T(8,128)S(1)} collective-permute-done((f32[72,128]{1,0:T(8,128)S(1)}, f32[72,128]{1,0:T(8,128)S(1)}, u32[]{:S(2)}, u32[]{:S(2)}) %collective-permute-start.1) | collective-permute-done | bytes 36896 | tf_op jit(solution)/shard_map/ppermute | solution.py:213
  10.1 3.8 %collective-permute-done.2 = f32[72,128]{1,0:T(8,128)S(1)} collective-permute-done((f32[72,128]{1,0:T(8,128)S(1)}, f32[72,128]{1,0:T(8,128)S(1)}, u32[]{:S(2)}, u32[]{:S(2)}) %collective-permute-start.2) | collective-permute-done | bytes 36896 | tf_op jit(solution)/shard_map/ppermute | solution.py:213
  13.9 0.0 collective-permute-done.3
  14.0 2.5 %collective-permute-start.4 = (f32[264,128]{1,0:T(8,128)S(1)}, f32[264,128]{1,0:T(8,128)S(1)}, u32[]{:S(2)}, u32[]{:S(2)}) collective-permute-start(f32[264,128]{1,0:T(8,128)S(1)} %concatenate.9.refs_0_), channel_id=1, source_target_pairs={{0,24},{8,16},{16,8},{24,0},{1,25},{9,17},{17,9},{25,1},{2,26},{10... | collective-permute-start | bytes 405512 | tf_op jit(solution)/shard_map/ppermute | solution.py:213
  16.5 0.5 %collective-permute-start.5 = (f32[264,128]{1,0:T(8,128)S(1)}, f32[264,128]{1,0:T(8,128)S(1)}, u32[]{:S(2)}, u32[]{:S(2)}) collective-permute-start(f32[264,128]{1,0:T(8,128)S(1)} %concatenate.9.refs_0_), channel_id=1, source_target_pairs={{0,16},{8,24},{16,0},{24,8},{1,17},{9,25},{17,1},{25,9},{2,18},{10... | collective-permute-start | bytes 405512 | tf_op jit(solution)/shard_map/ppermute | solution.py:213
  17.0 0.5 %collective-permute-start.6 = (f32[264,128]{1,0:T(8,128)S(1)}, f32[264,128]{1,0:T(8,128)S(1)}, u32[]{:S(2)}, u32[]{:S(2)}) collective-permute-start(f32[264,128]{1,0:T(8,128)S(1)} %concatenate.9.refs_0_), channel_id=1, source_target_pairs={{0,8},{8,0},{16,24},{24,16},{1,9},{9,1},{17,25},{25,17},{2,10},{10... | collective-permute-start | bytes 405512 | tf_op jit(solution)/shard_map/ppermute | solution.py:213
  17.5 1.6 %norms.1.refs_2_ = f32[64,128]{1,0:T(8,128)S(1)} custom-call(bf16[8192,128]{1,0:T(8,128)(2,1)S(1)} %get-tuple-element.9.x_ref), custom_call_target="tpu_custom_call" | custom-call | flops 2097152 | bytes 2097152 | tf_op jit(solution)/shard_map/norms/pallas_call | solution.py:100
  19.1 2.1 %collective-permute-done.4.refs_1_ = f32[264,128]{1,0:T(8,128)S(1)} collective-permute-done((f32[264,128]{1,0:T(8,128)S(1)}, f32[264,128]{1,0:T(8,128)S(1)}, u32[]{:S(2)}, u32[]{:S(2)}) %collective-permute-start.4) | collective-permute-done | bytes 135200 | tf_op jit(solution)/shard_map/ppermute | solution.py:213
  21.2 0.9 %collective-permute-done.5.refs_2_ = f32[264,128]{1,0:T(8,128)S(1)} collective-permute-done((f32[264,128]{1,0:T(8,128)S(1)}, f32[264,128]{1,0:T(8,128)S(1)}, u32[]{:S(2)}, u32[]{:S(2)}) %collective-permute-start.5) | collective-permute-done | bytes 135200 | tf_op jit(solution)/shard_map/ppermute | solution.py:213
  22.1 0.1 collective-permute-done.6.refs_3_
  22.1 0.9 %means.1.cent_ref.refs_0_ = bf16[512,128]{1,0:T(8,128)(2,1)S(1)} custom-call(f32[264,128]{1,0:T(8,128)S(1)} %concatenate.9.refs_0_, f32[264,128]{1,0:T(8,128)S(1)} %collective-permute-done.4.refs_1_, f32[264,128]{1,0:T(8,128)S(1)} %collective-permute-done.5.refs_2_, f32[264,128]{1,0:T(8,128)S(1)} %collective-permute-done.6.refs_3_), custom_call_target="tpu_custom_call" | custom-call | tf_op jit(solution)/shard_map/means/pallas_call | solution.py:143
  23.0 0.1 collective-permute-start.7
  23.1 2.4 %nearest_first.1.refs_1_ = f32[64,128]{1,0:T(8,128)S(1)} custom-call(bf16[512,128]{1,0:T(8,128)(2,1)S(1)} %means.1.cent_ref.refs_0_, bf16[8192,128]{1,0:T(8,128)(2,1)S(1)} %get-tuple-element.9.x_ref), custom_call_target="tpu_custom_call" | custom-call | flops 2147483648 | bytes 2097152 | tf_op jit(solution)/shard_map/nearest_first/pallas_call | solution.py:200
  25.6 0.0 collective-permute-done.7.cent_ref
  25.6 3.1 %nearest_last.1 = (bf16[128,128]{1,0:T(8,128)(2,1)}, f32[64,128]{1,0:T(8,128)}) custom-call(bf16[512,128]{1,0:T(8,128)(2,1)S(1)} %collective-permute-done.7.cent_ref, bf16[8192,128]{1,0:T(8,128)(2,1)S(1)} %get-tuple-element.9.x_ref, bf16[512,128]{1,0:T(8,128)(2,1)S(1)} %means.1.cent_ref.refs_0_, f32[64,128]{1,0:T(8,128)S(1)} %nearest_first.1.refs_1_, ...), custom_call_target="tpu_custom_call" | custom-call | flops 2147483648 | bytes 2097152 | tf_op jit(solution)/shard_map/nearest_last/pallas_call | solution.py:200
  (13 shorter events, 0.1 us)
Async XLA Ops:
  2.7 1.4 %collective-permute-start = (f32[40,128]{1,0:T(8,128)S(1)}, f32[40,128]{1,0:T(8,128)S(1)}, u32[]{:S(2)}, u32[]{:S(2)}) collective-permute-start(f32[40,128]{1,0:T(8,128)S(1)} %get-tuple-element.8), channel_id=1, source_target_pairs={{0,1},{1,0},{2,3},{3,2},{4,5},{5,4},{6,7},{7,6},{8,9},{9,8},{10,11... | collective-permute-start | bytes 61448 | tf_op jit(solution)/shard_map/ppermute | solution.py:213
  4.1 5.9 %collective-permute-start.1 = (f32[72,128]{1,0:T(8,128)S(1)}, f32[72,128]{1,0:T(8,128)S(1)}, u32[]{:S(2)}, u32[]{:S(2)}) collective-permute-start(f32[72,128]{1,0:T(8,128)S(1)} %pad_maximum_fusion), channel_id=1, source_target_pairs={{0,4},{1,5},{2,6},{3,7},{4,0},{5,1},{6,2},{7,3},{8,12},{9,13},{10,... | collective-permute-start | bytes 110600 | tf_op jit(solution)/shard_map/ppermute | solution.py:213
  8.1 5.8 %collective-permute-start.2 = (f32[72,128]{1,0:T(8,128)S(1)}, f32[72,128]{1,0:T(8,128)S(1)}, u32[]{:S(2)}, u32[]{:S(2)}) collective-permute-start(f32[72,128]{1,0:T(8,128)S(1)} %pad_maximum_fusion), channel_id=1, source_target_pairs={{0,6},{1,7},{2,4},{3,5},{4,2},{5,3},{6,0},{7,1},{8,14},{9,15},{10,... | collective-permute-start | bytes 110600 | tf_op jit(solution)/shard_map/ppermute | solution.py:213
  9.5 4.4 %collective-permute-start.3 = (f32[72,128]{1,0:T(8,128)S(1)}, f32[72,128]{1,0:T(8,128)S(1)}, u32[]{:S(2)}, u32[]{:S(2)}) collective-permute-start(f32[72,128]{1,0:T(8,128)S(1)} %pad_maximum_fusion), channel_id=1, source_target_pairs={{0,2},{1,3},{2,0},{3,1},{4,6},{5,7},{6,4},{7,5},{8,10},{9,11},{10,... | collective-permute-start | bytes 110600 | tf_op jit(solution)/shard_map/ppermute | solution.py:213
  14.0 7.2 %collective-permute-start.4 = (f32[264,128]{1,0:T(8,128)S(1)}, f32[264,128]{1,0:T(8,128)S(1)}, u32[]{:S(2)}, u32[]{:S(2)}) collective-permute-start(f32[264,128]{1,0:T(8,128)S(1)} %concatenate.9.refs_0_), channel_id=1, source_target_pairs={{0,24},{8,16},{16,8},{24,0},{1,25},{9,17},{17,9},{25,1},{2,26},{10... | collective-permute-start | bytes 405512 | tf_op jit(solution)/shard_map/ppermute | solution.py:213
  16.5 5.6 %collective-permute-start.5 = (f32[264,128]{1,0:T(8,128)S(1)}, f32[264,128]{1,0:T(8,128)S(1)}, u32[]{:S(2)}, u32[]{:S(2)}) collective-permute-start(f32[264,128]{1,0:T(8,128)S(1)} %concatenate.9.refs_0_), channel_id=1, source_target_pairs={{0,16},{8,24},{16,0},{24,8},{1,17},{9,25},{17,1},{25,9},{2,18},{10... | collective-permute-start | bytes 405512 | tf_op jit(solution)/shard_map/ppermute | solution.py:213
  17.0 5.1 %collective-permute-start.6 = (f32[264,128]{1,0:T(8,128)S(1)}, f32[264,128]{1,0:T(8,128)S(1)}, u32[]{:S(2)}, u32[]{:S(2)}) collective-permute-start(f32[264,128]{1,0:T(8,128)S(1)} %concatenate.9.refs_0_), channel_id=1, source_target_pairs={{0,8},{8,0},{16,24},{24,16},{1,9},{9,1},{17,25},{25,17},{2,10},{10... | collective-permute-start | bytes 405512 | tf_op jit(solution)/shard_map/ppermute | solution.py:213
  23.0 2.5 %collective-permute-start.7 = (bf16[512,128]{1,0:T(8,128)(2,1)S(1)}, bf16[512,128]{1,0:T(8,128)(2,1)S(1)}, u32[]{:S(2)}, u32[]{:S(2)}) collective-permute-start(bf16[512,128]{1,0:T(8,128)(2,1)S(1)} %means.1.cent_ref.refs_0_), channel_id=1, source_target_pairs={{0,1},{1,0},{2,3},{3,2},{4,5},{5,4},{6,7},{7,6},{8,9},{9,8},{10,11... | collective-permute-start | bytes 393224 | tf_op jit(solution)/shard_map/ppermute | solution.py:213
